TPU v7x, 32 devices: a whole 2x2x4 slice. The times are simulated.
32 devices in a mesh: grp: 2 (over x), seq: 16 (over z, y, core).
Axes of the slice: x: 2, y: 2, z: 4, core: 2. Of those that a mesh axis runs over, the one named last changes fastest.
Arguments:
- alignment: bfloat16 [64, 128, 768], P(('grp', 'seq')), parts along dimension 0, may hold values from -20 to 20
- protein_id: int32 [256], P('grp'), parts along dimension 0, may hold values from 0 to 3, never falling along the last dimension, each value on 1 to 64 neighbouring positions
- row_depth: int32 [8], P('grp'), parts along dimension 0, may hold values from 8 to 32, as said below
- row_gain: float32 [768], replicated, may hold values from 0.1 to 1.9
- row_query: bfloat16 [768, 768], replicated, may hold values from -40 to 40
- row_key: bfloat16 [768, 768], replicated, may hold values from -0.21875 to 0.21875
- row_value: bfloat16 [768, 768], replicated, may hold values from -0.21875 to 0.21875
- row_output: bfloat16 [768, 768], replicated, may hold values from -0.21875 to 0.21875
- column_gain: float32 [768], replicated, may hold values from 0.1 to 1.9
- column_query: bfloat16 [768, 768], replicated, may hold values from -40 to 40
- column_key: bfloat16 [768, 768], replicated, may hold values from -0.21875 to 0.21875
- column_value: bfloat16 [768, 768], replicated, may hold values from -0.21875 to 0.21875
- column_output: bfloat16 [768, 768], replicated, may hold values from -0.21875 to 0.21875
Outputs:
- layer_out: bfloat16 [64, 128, 768], P(('grp', 'seq')), parts along dimension 0
There are 2 independent parts, one for each index of `grp`. A program takes and returns all parts, laid end to end along the dimension named above; an argument that names none is the same for every part. Nothing has to cross between parts.
Inputs may be any that keep to these rules, and one draw needn't show every extreme that they name: `row_depth`: row 0 is real for every protein; one protein of each pack has all 32 rows real. `protein_id`: proteins occupy contiguous column ranges in order, each 1 to 64 columns.
All inputs are finite; a program needn't handle non-finite values.
Results may differ from a plain program's by a relative error of at most 0.011.
Values may be sent and summed in bfloat16 or wider, within the bound.
No kernel may reach another device: no remote copies, remote signals or barrier semaphores. Data moves between devices by JAX's collectives and lax.ppermute only.
A program may use at most 64 MiB of HBM per device.

v0:
```python
import math
import jax
import jax.numpy as jnp
from jax import lax
from jax.sharding import PartitionSpec as P

H = 12


def layer_norm(values, gain):
    full = values.astype(jnp.float32)
    middle = jnp.mean(full, axis=-1, keepdims=True)
    spread = jnp.mean((full - middle) ** 2, axis=-1, keepdims=True)
    return ((full - middle) * lax.rsqrt(spread + 1e-05) * gain).astype(jnp.bfloat16)


def project(normed, weight):
    shape = normed.shape
    flattened = normed.reshape(-1, shape[-1])
    return (
        jnp.dot(flattened, weight, preferred_element_type=jnp.float32)
        .astype(jnp.bfloat16)
        .reshape(shape[:-1] + (weight.shape[1],))
    )


def column_depth(protein_id, row_depth):
    onehot = protein_id[:, None] == jnp.arange(row_depth.shape[0], dtype=jnp.int32)[None, :]
    return jnp.sum(jnp.where(onehot, row_depth[None, :], 0), axis=1)


def per_device(
    alignment,
    protein_id,
    row_depth,
    row_gain,
    row_query,
    row_key,
    row_value,
    row_output,
    column_gain,
    column_query,
    column_key,
    column_value,
    column_output,
):
    rows_dev, columns, width = alignment.shape
    devices = lax.axis_size("seq")
    position = lax.axis_index("seq")
    total_rows = rows_dev * devices
    head_count = H
    head_size = width // head_count
    tile_cols = columns // devices
    depth_col = column_depth(protein_id, row_depth)
    row_ids = position * rows_dev + jnp.arange(rows_dev, dtype=jnp.int32)
    valid = row_ids[:, None] < depth_col[None, :]
    mask_bf = valid.astype(jnp.bfloat16)[:, :, None]
    normed_row = layer_norm(alignment, row_gain)
    query_a = (project(normed_row, row_query) * mask_bf).reshape(
        rows_dev, columns, head_count, head_size
    )
    key_a = (project(normed_row, row_key) * mask_bf).reshape(
        rows_dev, columns, head_count, head_size
    )
    value_a = project(normed_row, row_value).reshape(rows_dev, columns, head_count, head_size)
    scale = 1.0 / (math.sqrt(head_size) * math.sqrt(total_rows))
    tied = (
        lax.psum_scatter(
            jnp.einsum("rihe,rjhe->ihj", query_a, key_a, preferred_element_type=jnp.float32),
            "seq",
            scatter_dimension=0,
            tiled=True,
        )
        * scale
    )
    prot_query = lax.dynamic_slice_in_dim(protein_id, position * tile_cols, tile_cols, 0)
    same_prot = prot_query[:, None, None] == protein_id[None, None, :]
    tied = jnp.where(same_prot, tied, -1000000000.0)
    row_weights = jax.nn.softmax(tied, axis=-1).astype(jnp.bfloat16)
    row_mixed = (
        jnp.einsum(
            "ihj,rjhe->rihe",
            lax.all_gather(row_weights, "seq", axis=0, tiled=True),
            value_a,
            preferred_element_type=jnp.float32,
        )
        .astype(jnp.bfloat16)
        .reshape(rows_dev, columns, width)
    )
    after_row = (
        alignment.astype(jnp.float32)
        + jnp.dot(
            row_mixed.reshape(-1, width), row_output, preferred_element_type=jnp.float32
        ).reshape(rows_dev, columns, width)
    ).astype(jnp.bfloat16)
    normed_col = layer_norm(after_row, column_gain)
    moved = lax.all_to_all(normed_col, "seq", split_axis=1, concat_axis=0, tiled=True)
    query_b = project(moved, column_query)
    key_b = project(moved, column_key)
    value_b = project(moved, column_value)
    query_b = query_b.reshape(total_rows, tile_cols, head_count, head_size)
    key_b = key_b.reshape(total_rows, tile_cols, head_count, head_size)
    value_b = value_b.reshape(total_rows, tile_cols, head_count, head_size)
    depth_tile = lax.dynamic_slice_in_dim(depth_col, position * tile_cols, tile_cols, 0)
    key_valid = jnp.arange(total_rows, dtype=jnp.int32)[None, :] < depth_tile[:, None]
    col_scores = jnp.einsum(
        "rche,sche->chrs", query_b, key_b, preferred_element_type=jnp.float32
    ) / math.sqrt(head_size)
    col_scores = jnp.where(key_valid[:, None, None, :], col_scores, -1000000000.0)
    col_weights = jax.nn.softmax(col_scores, axis=-1).astype(jnp.bfloat16)
    col_mixed = jnp.einsum(
        "chrs,sche->rche", col_weights, value_b, preferred_element_type=jnp.float32
    ).astype(jnp.bfloat16)
    col_mixed = col_mixed.reshape(total_rows, tile_cols, width)
    returned = lax.all_to_all(col_mixed, "seq", split_axis=0, concat_axis=1, tiled=True)
    layer_out = after_row.astype(jnp.float32) + jnp.dot(
        returned.reshape(-1, width), column_output, preferred_element_type=jnp.float32
    ).reshape(rows_dev, columns, width)
    return layer_out.astype(jnp.bfloat16)


def solution(mesh):
    return jax.shard_map(
        per_device,
        mesh=mesh,
        in_specs=(
            P(("grp", "seq"), None, None),
            P("grp"),
            P("grp"),
            P(),
            P(),
            P(),
            P(),
            P(),
            P(),
            P(),
            P(),
            P(),
            P(),
        ),
        out_specs=P(("grp", "seq"), None, None),
        check_vma=False,
    )
```

profile of v0, /device:TPU:0, one launch (start us, length us, event | category | flops | bytes accessed | tf_op | source)
XLA Modules:
  0.0 158.1 jit_solution(10954076205752719301)
XLA Ops:
  6.5 1.3 convert_reduce_fusion
  7.8 1.2 fusion.15
  9.1 1.2 fusion.17
  11.1 1.7 %convolution_convert_fusion.4 = bf16[256,768]{1,0:T(8,128)(2,1)S(1)} fusion(bf16[256,768]{1,0:T(8,128)(2,1)S(1)} %bitcast.61, bf16[768,768]{1,0:T(8,128)(2,1)} %param.17), kind=kOutput, calls=%fused_computation.17 | convolution fusion | flops 302186496 | bytes 1966080 | tf_op jit(solution)/shard_map/dot_general | solution.py:21
  14.1 1.4 copy.79
  15.6 0.5 convolution_convert_fusion.6
  16.4 59.4 %reduce-scatter.2.cloned.1.call-done = f32[8,12,128]{2,1,0:T(8,128)} async-done(((f32[128,12,128]{2,1,0:T(8,128)}), f32[8,12,128]{2,1,0:T(8,128)}) %reduce-scatter.2.cloned.1.call-update) | async-done | bytes 49168 | tf_op jit(solution)/shard_map/reduce_scatter | solution.py:68
  75.8 1.0 fusion.38
  76.9 20.5 %all_gather.3 = bf16[128,12,128]{2,0,1:T(8,128)(2,1)S(1)} all-gather(bf16[8,12,128]{2,0,1:T(8,128)(2,1)S(1)} %copy.80), channel_id=1, replica_groups=mesh['grp'=2,'seq'=16] {'seq'}, dimensions={0}, use_global_device_ids=true | all-gather | bytes 417792 | tf_op jit(solution)/shard_map/all_gather | solution.py:83
  97.9 0.6 fusion.39
  99.0 1.2 copy.84
  100.1 3.6 %all-to-all-start = ((bf16[2,128,768]{2,0,1:T(2,128)(2,1)}), bf16[2,128,768]{2,0,1:T(2,128)(2,1)S(1)}, u32[]{:S(2)}, u32[]{:S(2)}) async-start(bf16[2,128,768]{2,0,1:T(2,128)(2,1)} %copy.84), calls=%async_computation.1 | async-start | bytes 786432 | tf_op jit(solution)/shard_map/all_to_all | solution.py:97
  103.8 12.0 %all-to-all-done = bf16[2,128,768]{2,0,1:T(2,128)(2,1)S(1)} async-done(((bf16[2,128,768]{2,0,1:T(2,128)(2,1)}), bf16[2,128,768]{2,0,1:T(2,128)(2,1)S(1)}, u32[]{:S(2)}, u32[]{:S(2)}) %all-to-all-start) | async-done | bytes 393248 | tf_op jit(solution)/shard_map/all_to_all | solution.py:97
  115.9 1.7 %convolution_convert_fusion.2 = bf16[256,768]{1,0:T(8,128)(2,1)S(1)} fusion(bf16[256,768]{1,0:T(8,128)(2,1)S(1)} %bitcast.63, bf16[768,768]{1,0:T(8,128)(2,1)} %param.22), kind=kOutput, calls=%fused_computation.15 | convolution fusion | flops 302186496 | bytes 1966080 | tf_op jit(solution)/shard_map/dot_general | solution.py:21
  117.7 1.6 %reshape_reshape.15 = bf16[32,8,12,64]{3,2,1,0:T(8,128)(2,1)} reshape(bf16[256,768]{1,0:T(8,128)(2,1)S(1)} %convolution_convert_fusion.2) | data formatting | bytes 786432 | tf_op jit(solution)/shard_map/reshape;reshape | solution.py:101
  119.3 1.7 %convolution_convert_fusion.1 = bf16[256,768]{1,0:T(8,128)(2,1)S(1)} fusion(bf16[256,768]{1,0:T(8,128)(2,1)S(1)} %bitcast.64, bf16[768,768]{1,0:T(8,128)(2,1)} %param.23), kind=kOutput, calls=%fused_computation.14 | convolution fusion | flops 302186496 | bytes 1966080 | tf_op jit(solution)/shard_map/dot_general | solution.py:21
  121.0 1.6 reshape_reshape.16
  122.6 1.7 %convolution_convert_fusion.3 = bf16[256,768]{1,0:T(8,128)(2,1)S(1)} fusion(bf16[256,768]{1,0:T(8,128)(2,1)S(1)} %bitcast.65, bf16[768,768]{1,0:T(8,128)(2,1)} %param.24), kind=kOutput, calls=%fused_computation.16 | convolution fusion | flops 302186496 | bytes 1966080 | tf_op jit(solution)/shard_map/dot_general | solution.py:21
  124.3 1.6 reshape_reshape.14
  125.9 4.2 %fusion.40 = (f32[8,12,32]{2,1,0:T(8,128)S(1)}, f32[8,12,32,32]{2,3,1,0:T(8,128)}) fusion(bf16[32,8,12,64]{3,2,1,0:T(8,128)(2,1)} %reshape_reshape.16, bf16[32,8,12,64]{3,2,1,0:T(8,128)(2,1)} %reshape_reshape.15, pred[8,32]{1,0:T(8,128)(4,1)S(1)} %iota_compare_fusion), kind=kOutput, calls=%fused_computation.68 | convolution fusion | flops 12976159 | bytes 1192192 | tf_op jit(solution)/shard_map/sub | solution.py:110
  130.1 2.1 %fusion.4 = bf16[32,8,12,64]{3,0,2,1:T(8,128)(2,1)S(1)} fusion(f32[8,12,32,32]{2,3,1,0:T(8,128)} %get-tuple-element.12, bf16[32,8,12,64]{3,2,1,0:T(8,128)(2,1)S(1)} %copy-done.4, f32[8,12,32]{2,1,0:T(8,128)S(1)} %get-tuple-element.11), kind=kOutput, calls=%fused_computation.7 | convolution fusion | flops 12976128 | bytes 1191936 | tf_op jit(solution)/shard_map/chrs,sche->rche/dot_general | solution.py:111
  132.6 0.6 reshape.144
  133.3 15.5 %all_to_all.30 = bf16[32,8,768]{2,1,0:T(8,128)(2,1)S(1)} all-to-all(bf16[32,8,768]{2,1,0:T(8,128)(2,1)S(1)} %reshape.144), channel_id=1, replica_groups=mesh['grp'=2,'seq'=16] {'seq'}, dimensions={0} | all-to-all | bytes 786432 | tf_op jit(solution)/shard_map/all_to_all | solution.py:115
  148.7 2.5 %fusion.7 = bf16[2,128,768]{2,1,0:T(8,128)(2,1)} fusion(f32[2,128,768]{2,1,0:T(8,128)S(1)} %get-tuple-element.10, bf16[768,768]{1,0:T(8,128)(2,1)} %param.25, bf16[2,16,8,768]{3,2,0,1:T(8,128)(2,1)S(1)} %bitcast.72), kind=kOutput, calls=%fused_computation.13 | convolution fusion | flops 302383104 | bytes 2752512 | tf_op jit(solution)/shard_map/dot_general | solution.py:116
  (48 shorter events, 3.9 us)
Async XLA Ops:
  6.5 91.4 %copy-start = (bf16[768,768]{1,0:T(8,128)(2,1)S(1)}, bf16[768,768]{1,0:T(8,128)(2,1)}, u32[]{:S(2)}) copy-start(bf16[768,768]{1,0:T(8,128)(2,1)} %param.20) | copy-start | bytes 3538948
  6.5 3.8 %copy-start.2 = (bf16[768,768]{1,0:T(8,128)(2,1)S(1)}, bf16[768,768]{1,0:T(8,128)(2,1)}, u32[]{:S(2)}) copy-start(bf16[768,768]{1,0:T(8,128)(2,1)} %param.18) | copy-start | bytes 3538948
  6.5 69.2 %reduce-scatter.2.cloned.1.call-start = ((), (), s32[]{:S(2)}) async-start(), calls=%async_computation.3 | async-start | bytes 1114112 | tf_op jit(solution)/shard_map/reduce_scatter | solution.py:68
  12.8 0.7 copy-start.6
  12.8 0.7 copy-start.7
  14.1 1.5 copy-start.3
  76.9 21.0 %copy-start.1 = (bf16[2,128,768]{2,1,0:T(8,128)(2,1)S(1)}, bf16[2,128,768]{2,1,0:T(8,128)(2,1)}, u32[]{:S(2)}) copy-start(bf16[2,128,768]{2,1,0:T(8,128)(2,1)} %param.13) | copy-start | bytes 1179652
  97.9 0.8 copy-start.5
  100.1 15.7 %all-to-all-start = ((bf16[2,128,768]{2,0,1:T(2,128)(2,1)}), bf16[2,128,768]{2,0,1:T(2,128)(2,1)S(1)}, u32[]{:S(2)}, u32[]{:S(2)}) async-start(bf16[2,128,768]{2,0,1:T(2,128)(2,1)} %copy.84), calls=%async_computation.1 | async-start | bytes 786432 | tf_op jit(solution)/shard_map/all_to_all | solution.py:97
  125.9 4.2 %copy-start.4 = (bf16[32,8,12,64]{3,2,1,0:T(8,128)(2,1)S(1)}, bf16[32,8,12,64]{3,2,1,0:T(8,128)(2,1)}, u32[]{:S(2)}) copy-start(bf16[32,8,12,64]{3,2,1,0:T(8,128)(2,1)} %reshape_reshape.14) | copy-start | bytes 1179652
Sparse Core Ops, SparseCore 0:
  15.6 60.1 reduce-scatter.1
where the time goes:
time: 159 us; the launch traced here: 158 us
  waiting for transfers between devices  71.4 us (45%)
  blocking collectives  36 us (23%)
  matrix products  18.1 us (11%)
  between operations  13.7 us (9%)
  local copies, waits for them, and re-layouts  9.7 us (6%)
  other arithmetic  5.64 us (4%)
  starting transfers between devices  3.56 us (2%)
    reduce_scatter x1, waiting for transfers between devices, per_device(): lax.psum_scatter(jnp.einsum('rihe,rjhe->ihj', query_a, key_a, preferred_e...  59.4 us
    all_gather x1, blocking collectives, per_device(): lax.all_gather(row_weights, 'seq', axis=0, tiled=True)  20.5 us
    all_to_all x1, blocking collectives, per_device(): lax.all_to_all(col_mixed, 'seq', split_axis=0, concat_axis=1, tiled=True)  15.5 us
    all_to_all x1, waiting for transfers between devices, per_device(): lax.all_to_all(normed_col, 'seq', split_axis=1, concat_axis=0, tiled=True)  12 us
    dot_general x6, matrix products, project(): jnp.dot(flattened, weight, preferred_element_type=jnp.float32)  7.94 us
    sub x1, matrix products, per_device(): col_weights = jax.nn.softmax(col_scores, axis=-1).astype(jnp.bfloat16)  4.24 us
    all_to_all x1, starting transfers between devices, per_device(): lax.all_to_all(normed_col, 'seq', split_axis=1, concat_axis=0, tiled=True)  3.55 us
  transfers between devices with their start and end apart: 2, of which 2 were waited for; matrix products, arithmetic and copies ran while one was open for 1% of the time, Pallas kernels for 0%

commit v1 on v0

--- a/solution.py
+++ b/solution.py
@@ -5,6 +5,12 @@
 from jax.sharding import PartitionSpec as P
 
 H = 12
+
+
+def swap_blocks(value, name, split, join):
+    pieces = jnp.split(value, lax.axis_size(name), axis=split)
+    received = lax.all_to_all(jnp.stack(pieces), name, 0, 0)
+    return jnp.concatenate(received, axis=join)
 
 
 def layer_norm(values, gain):
@@ -112,7 +118,7 @@
         "chrs,sche->rche", col_weights, value_b, preferred_element_type=jnp.float32
     ).astype(jnp.bfloat16)
     col_mixed = col_mixed.reshape(total_rows, tile_cols, width)
-    returned = lax.all_to_all(col_mixed, "seq", split_axis=0, concat_axis=1, tiled=True)
+    returned = swap_blocks(col_mixed, "seq", 0, 1)
     layer_out = after_row.astype(jnp.float32) + jnp.dot(
         returned.reshape(-1, width), column_output, preferred_element_type=jnp.float32
     ).reshape(rows_dev, columns, width)

time: 159 us -> 190 us (1.19)
  local copies, waits for them, and re-layouts: 9.7 us -> 42.3 us
    another operation x0 -> x17, local copies, waits for them, and re-layouts: none -> 14.8 us  [swap_blocks(): received = lax.all_to_all(jnp.stack(pieces), name, 0, 0)]
    unnamed x17 -> x34, local copies, waits for them, and re-layouts: 0.4 us -> 11.7 us
    split x0 -> x17, local copies, waits for them, and re-layouts: none -> 7.45 us  [swap_blocks(): pieces = jnp.split(value, lax.axis_size(name), axis=split)]
where the time goes in v1:
time: 190 us; the launch traced here: 188 us
  waiting for transfers between devices  69.9 us (37%)
  local copies, waits for them, and re-layouts  42.3 us (22%)
  blocking collectives  36 us (19%)
  matrix products  16.8 us (9%)
  between operations  13.7 us (7%)
  other arithmetic  5.64 us (3%)
  starting transfers between devices  3.74 us (2%)
    reduce_scatter x1, waiting for transfers between devices, per_device(): lax.psum_scatter(jnp.einsum('rihe,rjhe->ihj', query_a, key_a, preferred_e...  58.1 us
    all_gather x1, blocking collectives, per_device(): lax.all_gather(row_weights, 'seq', axis=0, tiled=True)  20.5 us
    all_to_all x1, blocking collectives, swap_blocks(): received = lax.all_to_all(jnp.stack(pieces), name, 0, 0)  15.5 us
    another operation x17, local copies, waits for them, and re-layouts, swap_blocks(): received = lax.all_to_all(jnp.stack(pieces), name, 0, 0)  14.8 us
    all_to_all x1, waiting for transfers between devices, per_device(): lax.all_to_all(normed_col, 'seq', split_axis=1, concat_axis=0, tiled=True)  11.8 us
    unnamed x34, local copies, waits for them, and re-layouts  11.7 us
    dot_general x6, matrix products, project(): jnp.dot(flattened, weight, preferred_element_type=jnp.float32)  7.94 us
    split x17, local copies, waits for them, and re-layouts, swap_blocks(): pieces = jnp.split(value, lax.axis_size(name), axis=split)  7.45 us
  transfers between devices with their start and end apart: 2, of which 2 were waited for; matrix products, arithmetic and copies ran while one was open for 1% of the time, Pallas kernels for 0%

profile of v1, /device:TPU:0, one launch (start us, length us, event | category | flops | bytes accessed | tf_op | source)
XLA Modules:
  0.0 188.2 jit_solution(1822983468582941143)
XLA Ops:
  13.8 1.4 copy.124
  15.3 1.7 convolution_convert_fusion.6
  17.4 58.1 %reduce-scatter.2.cloned.1.call-done = f32[8,12,128]{2,1,0:T(8,128)} async-done(((f32[128,12,128]{2,1,0:T(8,128)}), f32[8,12,128]{2,1,0:T(8,128)}) %reduce-scatter.2.cloned.1.call-update) | async-done | bytes 49168 | tf_op jit(solution)/shard_map/reduce_scatter | solution.py:74
  76.6 20.5 %all_gather.3 = bf16[128,12,128]{2,0,1:T(8,128)(2,1)S(1)} all-gather(bf16[8,12,128]{2,0,1:T(8,128)(2,1)S(1)} %copy.125), channel_id=1, replica_groups=mesh['grp'=2,'seq'=16] {'seq'}, dimensions={0}, use_global_device_ids=true | all-gather | bytes 417792 | tf_op jit(solution)/shard_map/all_gather | solution.py:89
  99.8 3.7 %all-to-all-start = ((bf16[2,128,768]{2,0,1:T(2,128)(2,1)}), bf16[2,128,768]{2,0,1:T(2,128)(2,1)S(1)}, u32[]{:S(2)}, u32[]{:S(2)}) async-start(bf16[2,128,768]{2,0,1:T(2,128)(2,1)} %copy.129), calls=%async_computation.1 | async-start | bytes 786432 | tf_op jit(solution)/shard_map/all_to_all | solution.py:103
  103.7 11.8 %all-to-all-done = bf16[2,128,768]{2,0,1:T(2,128)(2,1)S(1)} async-done(((bf16[2,128,768]{2,0,1:T(2,128)(2,1)}), bf16[2,128,768]{2,0,1:T(2,128)(2,1)S(1)}, u32[]{:S(2)}, u32[]{:S(2)}) %all-to-all-start) | async-done | bytes 393248 | tf_op jit(solution)/shard_map/all_to_all | solution.py:103
  115.6 1.7 convolution_convert_fusion.2
  117.4 1.6 reshape_reshape.16
  119.0 1.7 convolution_convert_fusion.1
  120.7 1.6 reshape_reshape.17
  122.3 1.7 convolution_convert_fusion.3
  124.0 1.6 reshape_reshape.15
  125.6 4.2 %fusion.41 = (f32[8,12,32]{2,1,0:T(8,128)S(1)}, f32[8,12,32,32]{2,3,1,0:T(8,128)}) fusion(bf16[32,8,12,64]{3,2,1,0:T(8,128)(2,1)} %reshape_reshape.17, bf16[32,8,12,64]{3,2,1,0:T(8,128)(2,1)} %reshape_reshape.16, pred[8,32]{1,0:T(8,128)(4,1)S(1)} %iota_compare_fusion), kind=kOutput, calls=%fused_computation.85 | convolution fusion | flops 12976159 | bytes 1192192 | tf_op jit(solution)/shard_map/sub | solution.py:116
  129.8 2.1 %fusion.4 = bf16[32,8,12,64]{3,0,2,1:T(8,128)(2,1)S(1)} fusion(f32[8,12,32,32]{2,3,1,0:T(8,128)} %get-tuple-element.28, bf16[32,8,12,64]{3,2,1,0:T(8,128)(2,1)S(1)} %copy-done.5, f32[8,12,32]{2,1,0:T(8,128)S(1)} %get-tuple-element.27), kind=kOutput, calls=%fused_computation.7 | convolution fusion | flops 12976128 | bytes 1191936 | tf_op jit(solution)/shard_map/chrs,sche->rche/dot_general | solution.py:117
  132.0 1.5 fusion.38
  141.5 1.5 copy.148
  143.1 1.5 stack.63
  144.6 1.4 copy.149
  146.1 1.5 stack.64
  147.6 1.4 copy.150
  149.0 1.6 stack.65
  150.6 1.4 copy.151
  152.0 1.5 stack.66
  164.7 15.5 %all_to_all.20 = bf16[16,2,8,768]{3,2,1,0:T(8,128)(2,1)S(1)} all-to-all(bf16[16,2,8,768]{3,2,1,0:T(8,128)(2,1)S(1)} %constant_dynamic-update-slice_fusion), channel_id=1, replica_groups=mesh['grp'=2,'seq'=16] {'seq'}, dimensions={0} | all-to-all | bytes 786432 | tf_op jit(solution)/shard_map/all_to_all | solution.py:12
  (97 shorter events, 31.8 us)
Async XLA Ops:
  6.5 91.1 %copy-start = (bf16[768,768]{1,0:T(8,128)(2,1)S(1)}, bf16[768,768]{1,0:T(8,128)(2,1)}, u32[]{:S(2)}) copy-start(bf16[768,768]{1,0:T(8,128)(2,1)} %param.20) | copy-start | bytes 3538948
  6.5 3.8 %copy-start.2 = (bf16[768,768]{1,0:T(8,128)(2,1)S(1)}, bf16[768,768]{1,0:T(8,128)(2,1)}, u32[]{:S(2)}) copy-start(bf16[768,768]{1,0:T(8,128)(2,1)} %param.18) | copy-start | bytes 3538948
  6.5 68.9 %reduce-scatter.2.cloned.1.call-start = ((), (), s32[]{:S(2)}) async-start(), calls=%async_computation.3 | async-start | bytes 1114112 | tf_op jit(solution)/shard_map/reduce_scatter | solution.py:74
  10.8 1.3 copy-start.3
  12.6 0.7 copy-start.7
  12.6 0.7 copy-start.8
  76.6 21.0 %copy-start.1 = (bf16[2,128,768]{2,1,0:T(8,128)(2,1)S(1)}, bf16[2,128,768]{2,1,0:T(8,128)(2,1)}, u32[]{:S(2)}) copy-start(bf16[2,128,768]{2,1,0:T(8,128)(2,1)} %param.13) | copy-start | bytes 1179652
  97.6 0.8 copy-start.6
  99.8 15.7 %all-to-all-start = ((bf16[2,128,768]{2,0,1:T(2,128)(2,1)}), bf16[2,128,768]{2,0,1:T(2,128)(2,1)S(1)}, u32[]{:S(2)}, u32[]{:S(2)}) async-start(bf16[2,128,768]{2,0,1:T(2,128)(2,1)} %copy.129), calls=%async_computation.1 | async-start | bytes 786432 | tf_op jit(solution)/shard_map/all_to_all | solution.py:103
  125.6 4.2 %copy-start.5 = (bf16[32,8,12,64]{3,2,1,0:T(8,128)(2,1)S(1)}, bf16[32,8,12,64]{3,2,1,0:T(8,128)(2,1)}, u32[]{:S(2)}) copy-start(bf16[32,8,12,64]{3,2,1,0:T(8,128)(2,1)} %reshape_reshape.15) | copy-start | bytes 1179652
  141.5 38.6 %copy-start.4 = (bf16[768,768]{1,0:T(8,128)(2,1)S(1)}, bf16[768,768]{1,0:T(8,128)(2,1)}, u32[]{:S(2)}) copy-start(bf16[768,768]{1,0:T(8,128)(2,1)} %param.25) | copy-start | bytes 3538948
Sparse Core Ops, SparseCore 0:
  15.3 60.1 reduce-scatter.1
